TPU v7x, 32 devices: a whole 2x2x4 slice. The times are simulated.
32 devices in a mesh: team: 2 (over x), blk: 4 (over z), head: 4 (over y, core).
Axes of the slice: x: 2, y: 2, z: 4, core: 2. Of those that a mesh axis runs over, the one named last changes fastest.
Arguments:
- queries: bfloat16 [1024, 8, 8, 128], P('blk', 'head', 'team'), may hold values from -40 to 40
- features: bfloat16 [1024, 8192], P('blk', ('team', 'head')), may hold values from -6 to 6
- adapter_down: bfloat16 [4, 8192, 64], P(None, ('team', 'head')), may hold values from -0.0625 to 0.0625
- adapter_key_up: bfloat16 [4, 64, 8, 128], P(None, None, 'head'), may hold values from -0.75 to 0.75
- adapter_value_up: bfloat16 [4, 64, 8, 128], P(None, None, 'head'), may hold values from -0.75 to 0.75
- base_key: bfloat16 [1024, 8, 128], P('blk', 'head'), may hold values from -6 to 6
- base_value: bfloat16 [1024, 8, 128], P('blk', 'head'), may hold values from -24 to 24
- prefix_key: bfloat16 [2048, 8, 128], P('blk', 'head'), may hold values from -7 to 7
- prefix_value: bfloat16 [2048, 8, 128], P('blk', 'head'), may hold values from -24 to 24
- adapter_ids: int32 [4], replicated, may hold values from 0 to 3
- block_order: int32 [4], replicated, may hold values from 0 to 15
Outputs:
- attended: bfloat16 [1024, 8, 8, 128], P('blk', 'head', 'team')
All inputs are finite; a program needn't handle non-finite values.
Results may differ from a plain program's by a relative error of at most 0.011.
Values may be sent and summed in bfloat16 or wider, within the bound.
No kernel may reach another device: no remote copies, remote signals or barrier semaphores. Data moves between devices by JAX's collectives and lax.ppermute only.
A program may use at most 64 MiB of HBM per device.

v0:
```python
import math
import jax
import jax.numpy as jnp
from jax import lax
from jax.sharding import PartitionSpec as P

NEG_FILL = -1e30


def block_length(row_count):
    for candidate in range(min(row_count, 1024), 0, -1):
        if row_count % candidate == 0:
            return candidate
    return row_count


def key_positions(row_count, shard_rows, prefix_dev, query_dev, block_order, block_count):
    row_index = jnp.arange(row_count, dtype=jnp.int32)
    holder = row_index // shard_rows
    within = row_index - holder * shard_rows
    block_ids = jnp.arange(block_count, dtype=jnp.int32)
    holder_order = jnp.sum(
        jnp.where(holder[:, None] == block_ids[None, :], block_order[None, :], 0), axis=1
    )
    later = prefix_dev * block_count + holder_order * query_dev + within - prefix_dev
    return jnp.where(within < prefix_dev, holder * prefix_dev + within, later)


def attend(running, query_rows, query_pos, key_rows, value_rows, key_pos):
    row_count = key_rows.shape[0]
    block_rows = block_length(row_count)
    key_blocks = row_count // block_rows
    kv_heads = key_rows.shape[1]
    head_dim = key_rows.shape[2]
    score_scale = 1.0 / math.sqrt(head_dim)
    latest = jnp.max(query_pos)
    key_split = key_rows.reshape((key_blocks, block_rows, kv_heads, head_dim))
    value_split = value_rows.reshape((key_blocks, block_rows, kv_heads, head_dim))
    pos_split = key_pos.reshape((key_blocks, block_rows))

    def advance(carried, block_data):
        block_keys, block_values, block_pos = block_data

        def compute(previous):
            row_max, row_sum, weighted = previous
            scores = (
                jnp.einsum(
                    "tkgd,skd->kgts", query_rows, block_keys, preferred_element_type=jnp.float32
                )
                * score_scale
            )
            visible = block_pos[None, None, None, :] <= query_pos[None, None, :, None]
            scores = jnp.where(visible, scores, NEG_FILL)
            new_max = jnp.maximum(row_max, jnp.max(scores, axis=-1))
            weights = jnp.where(visible, jnp.exp(scores - new_max[..., None]), 0.0)
            factor = jnp.exp(row_max - new_max)
            row_sum = row_sum * factor + jnp.sum(weights, axis=-1)
            product = jnp.einsum(
                "kgts,skd->kgtd",
                weights.astype(jnp.bfloat16),
                block_values,
                preferred_element_type=jnp.float32,
            )
            weighted = weighted * factor[..., None] + product
            return (new_max, row_sum, weighted)

        return (lax.cond(jnp.min(block_pos) > latest, lambda kept: kept, compute, carried), None)

    result, _ = lax.scan(advance, running, (key_split, value_split, pos_split))
    return result


def on_device(
    queries,
    features,
    adapter_down,
    adapter_key_up,
    adapter_value_up,
    base_key,
    base_value,
    prefix_key,
    prefix_value,
    adapter_ids,
    block_order,
):
    block_count = lax.axis_size("blk")
    my_block = lax.axis_index("blk")
    query_dev = queries.shape[0]
    kv_heads = queries.shape[1]
    group_dev = queries.shape[2]
    head_dim = queries.shape[3]
    prefix_dev = prefix_key.shape[0]
    rank_width = adapter_down.shape[2]
    shard_rows = prefix_dev + query_dev
    chosen = adapter_ids[my_block]
    down_rows = lax.dynamic_index_in_dim(adapter_down, chosen, 0, keepdims=False)
    partial_latent = jnp.dot(features, down_rows, preferred_element_type=jnp.float32)
    latent = lax.psum(partial_latent, ("team", "head")).astype(jnp.bfloat16)

    def expand(up_table, base_rows):
        up_rows = lax.dynamic_index_in_dim(up_table, chosen, 0, keepdims=False).reshape(
            rank_width, kv_heads * head_dim
        )
        delta = jnp.dot(latent, up_rows, preferred_element_type=jnp.float32).reshape(
            query_dev, kv_heads, head_dim
        )
        return (base_rows.astype(jnp.float32) + delta).astype(jnp.bfloat16)

    key_rows = jnp.concatenate([prefix_key, expand(adapter_key_up, base_key)], axis=0)
    value_rows = jnp.concatenate([prefix_value, expand(adapter_value_up, base_value)], axis=0)
    prefix_total = prefix_dev * block_count
    offsets = jnp.arange(query_dev, dtype=jnp.int32)
    query_pos = prefix_total + block_order[my_block] * query_dev + offsets
    initial = (
        jnp.full((kv_heads, group_dev, query_dev), NEG_FILL, jnp.float32),
        jnp.zeros((kv_heads, group_dev, query_dev), jnp.float32),
        jnp.zeros((kv_heads, group_dev, query_dev, head_dim), jnp.float32),
    )
    key_piece = lax.all_gather(key_rows, "blk", axis=0, tiled=True)
    value_piece = lax.all_gather(value_rows, "blk", axis=0, tiled=True)
    piece_pos = key_positions(
        key_piece.shape[0], shard_rows, prefix_dev, query_dev, block_order, block_count
    )
    row_max, row_sum, weighted = attend(
        initial, queries, query_pos, key_piece, value_piece, piece_pos
    )
    result = weighted / row_sum[..., None]
    return result.transpose(2, 0, 1, 3).astype(jnp.bfloat16)


def solution(mesh):
    placed = (
        P("blk", "head", "team", None),
        P("blk", ("team", "head")),
        P(None, ("team", "head"), None),
        P(None, None, "head", None),
        P(None, None, "head", None),
        P("blk", "head", None),
        P("blk", "head", None),
        P("blk", "head", None),
        P("blk", "head", None),
        P(),
        P(),
    )
    return jax.shard_map(
        on_device,
        mesh=mesh,
        in_specs=placed,
        out_specs=P("blk", "head", "team", None),
        check_vma=False,
    )
```

profile of v0, /device:TPU:0, one launch (start us, length us, event | category | flops | bytes accessed | tf_op | source)
XLA Modules:
  0.0 160.4 jit_solution(10820601032562232662)
XLA Ops:
  6.5 1.3 dynamic_slice.39
  9.8 1.2 convolution_bitcast_fusion
  11.0 26.0 %psum.7 = bf16[256,64]{0,1:T(8,128)(2,1)S(1)} all-reduce(f32[256,64]{0,1:T(8,128)S(1)} %convolution_bitcast_fusion), channel_id=1, replica_groups=mesh['team'=2,'blk'=4,'head'=4] {'team','head'}, use_global_device_ids=true, to_apply=%region_0.1 | all-reduce | flops 16384 | bytes 98304 | tf_op jit(solution)/shard_map/psum | solution.py:98
  37.0 1.0 copy.35
  38.0 0.8 constant_dynamic-slice_fusion.1
  38.8 1.1 fusion.21
  39.9 0.8 pad_maximum_fusion
  40.7 0.0 all-gather.3.cloned.1.call-update
  40.7 0.0 all-gather.5.cloned.1.call-start
  40.8 1.0 copy.38
  41.8 1.1 fusion.22
  42.9 0.8 pad_maximum_fusion.1
  43.6 0.0 all-gather.5.cloned.1.call-update
  43.7 1.2 dynamic_slice.38
  45.5 0.6 add_reduce_fusion
  46.1 1.1 copy.40
  47.2 0.8 select_reduce_fusion
  48.1 29.3 %all-gather.3.cloned.1.call-done = bf16[3072,2,128]{2,0,1:T(8,128)(2,1)} async-done(((bf16[768,2,128]{2,0,1:T(8,128)(2,1)}), bf16[3072,2,128]{2,0,1:T(8,128)(2,1)}) %all-gather.3.cloned.1.call-update) | async-done | bytes 1572880 | tf_op jit(solution)/shard_map/all_gather | solution.py:119
  77.4 1.5 copy.39
  78.9 36.0 %all-gather.5.cloned.1.call-done = bf16[3072,2,128]{2,0,1:T(8,128)(2,1)} async-done(((bf16[768,2,128]{2,0,1:T(8,128)(2,1)}), bf16[3072,2,128]{2,0,1:T(8,128)(2,1)}) %all-gather.5.cloned.1.call-update) | async-done | bytes 1572880 | tf_op jit(solution)/shard_map/all_gather | solution.py:120
  114.9 2.7 %copy.41 = bf16[3,1024,2,128]{3,1,2,0:T(8,128)(2,1)} copy(bf16[3,1024,2,128]{3,1,0,2:T(8,128)(2,1)} %bitcast.83) | data formatting | bytes 3145728
  117.6 1.0 broadcast_in_dim.56
  118.6 31.8 %while.15 = (s32[]{:T(128)}, f32[2,4,256]{2,1,0:T(4,128)S(1)}, f32[2,4,256]{2,1,0:T(4,128)S(1)}, f32[2,4,256,128]{3,2,1,0:T(8,128)}, s32[3,1024]{1,0:T(4,128)S(1...) while((s32[]{:T(128)}, f32[2,4,256]{2,1,0:T(4,128)S(1)}, ...), condition=%wide.region_9.10_spmd.clone, body=%wide.region_3.9_spmd.clone.sunk | while | flops 1101796608 | bytes 38421312 | solution.py:69
  118.6 0.6 fusion.45
  120.5 8.7 %conditional.3 = (f32[2,4,256]{2,1,0:T(4,128)S(1)}, f32[2,4,256]{2,1,0:T(4,128)S(1)}, f32[2,4,256,128]{3,2,1,0:T(8,128)}) conditional(s32[]{:T(128)} %convert_element_type.57, (s32[1,1024]{1,0:T(1,128)S(1)}, s32[]{:T(128)}, bf16[3,1024,2,128]{3,1,2,0:T(8,128)(2,1)S(1)}, s32[]{:T(128)}, bf16[256,2,4,128]{3,0,2,1:T(8,128)(2,1)S(1)}, ...), branch_computations={%region_5.7_spmd, %region_8.8_spmd} | conditional | flops 1101795584 | bytes 38395480 | solution.py:67
  120.5 0.2 broadcast_compare_fusion
  120.7 0.0 copy-start.1
  120.7 1.4 fusion.2
  122.2 2.0 %fusion.4 = f32[2,4,256]{2,1,0:T(4,128)S(1)} fusion(f32[2,1024,256,4]{2,1,3,0:T(8,128)S(1)} %get-tuple-element.228, f32[2,4,256]{2,1,0:T(4,128)S(1)} %max.4, pred[256,1024]{0,1:T(8,128)(4,1)S(1)} %broadcast_compare_fusion), kind=kLoop, calls=%fused_computation.5 | loop fusion | flops 10483712 | bytes 8667136 | tf_op jit(solution)/shard_map/while/body/eval_jaxpr/cond/branch_0_fun/reduce_sum | solution.py:57
  124.2 4.0 %fusion.8 = f32[2,4,256,128]{3,2,1,0:T(8,128)S(1)} fusion(f32[2,1024,256,4]{2,1,3,0:T(8,128)S(1)} %get-tuple-element.228, f32[2,4,256]{2,1,0:T(4,128)S(1)} %max.4, pred[256,1024]{0,1:T(8,128)(4,1)S(1)} %broadcast_compare_fusion, f32[2,4,256,128]{3,2,1,0:T(8,128)S(1)} %copy-done.1, bf16[3,1024,2,128]{3,1,2,0:T(8,128)(2,1)} %get-tuple-element.125, ...), kind=kOutput, calls=%fused_computation.8 | convolution fusion | flops 547880960 | bytes 11289088 | tf_op jit(solution)/shard_map/while/body/eval_jaxpr/cond/branch_0_fun/kgts,skd->kgtd/dot_general | solution.py:58
  128.3 1.0 copy-done.2
  129.2 0.6 fusion.45
  131.1 8.7 %conditional.3 = (f32[2,4,256]{2,1,0:T(4,128)S(1)}, f32[2,4,256]{2,1,0:T(4,128)S(1)}, f32[2,4,256,128]{3,2,1,0:T(8,128)}) conditional(s32[]{:T(128)} %convert_element_type.57, (s32[1,1024]{1,0:T(1,128)S(1)}, s32[]{:T(128)}, bf16[3,1024,2,128]{3,1,2,0:T(8,128)(2,1)S(1)}, s32[]{:T(128)}, bf16[256,2,4,128]{3,0,2,1:T(8,128)(2,1)S(1)}, ...), branch_computations={%region_5.7_spmd, %region_8.8_spmd} | conditional | flops 1101795584 | bytes 38395480 | solution.py:67
  131.1 0.2 broadcast_compare_fusion
  131.3 0.0 copy-start.1
  131.3 1.4 fusion.2
  132.8 2.0 %fusion.4 = f32[2,4,256]{2,1,0:T(4,128)S(1)} fusion(f32[2,1024,256,4]{2,1,3,0:T(8,128)S(1)} %get-tuple-element.228, f32[2,4,256]{2,1,0:T(4,128)S(1)} %max.4, pred[256,1024]{0,1:T(8,128)(4,1)S(1)} %broadcast_compare_fusion), kind=kLoop, calls=%fused_computation.5 | loop fusion | flops 10483712 | bytes 8667136 | tf_op jit(solution)/shard_map/while/body/eval_jaxpr/cond/branch_0_fun/reduce_sum | solution.py:57
  134.8 4.0 %fusion.8 = f32[2,4,256,128]{3,2,1,0:T(8,128)S(1)} fusion(f32[2,1024,256,4]{2,1,3,0:T(8,128)S(1)} %get-tuple-element.228, f32[2,4,256]{2,1,0:T(4,128)S(1)} %max.4, pred[256,1024]{0,1:T(8,128)(4,1)S(1)} %broadcast_compare_fusion, f32[2,4,256,128]{3,2,1,0:T(8,128)S(1)} %copy-done.1, bf16[3,1024,2,128]{3,1,2,0:T(8,128)(2,1)} %get-tuple-element.125, ...), kind=kOutput, calls=%fused_computation.8 | convolution fusion | flops 547880960 | bytes 11289088 | tf_op jit(solution)/shard_map/while/body/eval_jaxpr/cond/branch_0_fun/kgts,skd->kgtd/dot_general | solution.py:58
  138.9 1.0 copy-done.2
  139.8 0.6 fusion.45
  141.7 8.7 %conditional.3 = (f32[2,4,256]{2,1,0:T(4,128)S(1)}, f32[2,4,256]{2,1,0:T(4,128)S(1)}, f32[2,4,256,128]{3,2,1,0:T(8,128)}) conditional(s32[]{:T(128)} %convert_element_type.57, (s32[1,1024]{1,0:T(1,128)S(1)}, s32[]{:T(128)}, bf16[3,1024,2,128]{3,1,2,0:T(8,128)(2,1)S(1)}, s32[]{:T(128)}, bf16[256,2,4,128]{3,0,2,1:T(8,128)(2,1)S(1)}, ...), branch_computations={%region_5.7_spmd, %region_8.8_spmd} | conditional | flops 1101795584 | bytes 38395480 | solution.py:67
  141.7 0.2 broadcast_compare_fusion
  141.9 1.4 fusion.2
  143.4 2.0 %fusion.4 = f32[2,4,256]{2,1,0:T(4,128)S(1)} fusion(f32[2,1024,256,4]{2,1,3,0:T(8,128)S(1)} %get-tuple-element.228, f32[2,4,256]{2,1,0:T(4,128)S(1)} %max.4, pred[256,1024]{0,1:T(8,128)(4,1)S(1)} %broadcast_compare_fusion), kind=kLoop, calls=%fused_computation.5 | loop fusion | flops 10483712 | bytes 8667136 | tf_op jit(solution)/shard_map/while/body/eval_jaxpr/cond/branch_0_fun/reduce_sum | solution.py:57
  145.4 4.0 %fusion.8 = f32[2,4,256,128]{3,2,1,0:T(8,128)S(1)} fusion(f32[2,1024,256,4]{2,1,3,0:T(8,128)S(1)} %get-tuple-element.228, f32[2,4,256]{2,1,0:T(4,128)S(1)} %max.4, pred[256,1024]{0,1:T(8,128)(4,1)S(1)} %broadcast_compare_fusion, f32[2,4,256,128]{3,2,1,0:T(8,128)S(1)} %copy-done.1, bf16[3,1024,2,128]{3,1,2,0:T(8,128)(2,1)} %get-tuple-element.125, ...), kind=kOutput, calls=%fused_computation.8 | convolution fusion | flops 547880960 | bytes 11289088 | tf_op jit(solution)/shard_map/while/body/eval_jaxpr/cond/branch_0_fun/kgts,skd->kgtd/dot_general | solution.py:58
  149.5 1.0 copy-done.2
  150.4 0.2 copy.42
  150.6 2.9 %fusion.24 = bf16[256,2,4,128]{3,2,1,0:T(4,128)(2,1)} fusion(f32[2,4,256]{1,0,2:T(2,128)S(1)} %copy.42, f32[2,4,256,128]{3,2,1,0:T(8,128)} %get-tuple-element.142), kind=kLoop, calls=%fused_computation.31 | loop fusion | flops 524288 | bytes 1581056 | tf_op jit(solution)/shard_map/convert_element_type | solution.py:128
  (31 shorter events, 0.2 us)
Async XLA Ops:
  6.5 3.2 %copy-start = (bf16[256,1024]{1,0:T(8,128)(2,1)S(1)}, bf16[256,1024]{1,0:T(8,128)(2,1)}, u32[]{:S(2)}) copy-start(bf16[256,1024]{1,0:T(8,128)(2,1)} %param.16) | copy-start | bytes 1572868
  6.5 70.8 %all-gather.3.cloned.1.call-start = ((), (), s32[]{:S(2)}) async-start(), calls=%async_computation | async-start | bytes 1966080 | tf_op jit(solution)/shard_map/all_gather | solution.py:119
  40.7 74.2 %all-gather.5.cloned.1.call-start = ((), (), s32[]{:S(2)}) async-start(), calls=%async_computation.1 | async-start | bytes 1966080 | tf_op jit(solution)/shard_map/all_gather | solution.py:120
  120.7 3.5 %copy-start.1 = (f32[2,4,256,128]{3,2,1,0:T(8,128)S(1)}, f32[2,4,256,128]{3,2,1,0:T(8,128)}, u32[]{:S(2)}) copy-start(f32[2,4,256,128]{3,2,1,0:T(8,128)} %get-tuple-element.124) | copy-start | bytes 3145732 | tf_op jit(solution)/shard_map/while/body/eval_jaxpr/cond
  128.3 1.0 copy-start.2
  131.3 3.5 %copy-start.1 = (f32[2,4,256,128]{3,2,1,0:T(8,128)S(1)}, f32[2,4,256,128]{3,2,1,0:T(8,128)}, u32[]{:S(2)}) copy-start(f32[2,4,256,128]{3,2,1,0:T(8,128)} %get-tuple-element.124) | copy-start | bytes 3145732 | tf_op jit(solution)/shard_map/while/body/eval_jaxpr/cond
  138.9 1.0 copy-start.2
  141.9 3.5 %copy-start.1 = (f32[2,4,256,128]{3,2,1,0:T(8,128)S(1)}, f32[2,4,256,128]{3,2,1,0:T(8,128)}, u32[]{:S(2)}) copy-start(f32[2,4,256,128]{3,2,1,0:T(8,128)} %get-tuple-element.124) | copy-start | bytes 3145732 | tf_op jit(solution)/shard_map/while/body/eval_jaxpr/cond
  149.5 1.0 copy-start.2
Sparse Core Ops, SparseCore 0:
  40.8 36.4 all-gather.2
  78.9 35.9 all-gather.4
where the time goes:
time: 161 us; the launch traced here: 160 us
  waiting for transfers between devices  65.4 us (41%)
  blocking collectives  26 us (16%)
  matrix products  19.7 us (12%)
  between operations  16 us (10%)
  local copies, waits for them, and re-layouts  14.8 us (9%)
  other arithmetic  14.6 us (9%)
  loops' own time  3.9 us (2%)
    all_gather x1, waiting for transfers between devices, on_device(): value_piece = lax.all_gather(value_rows, 'blk', axis=0, tiled=True)  36 us
    all_gather x1, waiting for transfers between devices, on_device(): key_piece = lax.all_gather(key_rows, 'blk', axis=0, tiled=True)  29.3 us
    psum x1, blocking collectives, on_device(): latent = lax.psum(partial_latent, ('team', 'head')).astype(jnp.bfloat16)  26 us
    dot_general x3, matrix products, compute(): jnp.einsum('kgts,skd->kgtd', weights.astype(jnp.bfloat16), block_values,...  12.1 us
    unnamed x7, local copies, waits for them, and re-layouts  7.28 us
    reduce_sum x3, other arithmetic, compute(): row_sum = row_sum * factor + jnp.sum(weights, axis=-1)  6.09 us
    dot_general x3, matrix products, compute(): jnp.einsum('tkgd,skd->kgts', query_rows, block_keys, preferred_element_ty...  4.2 us
    another operation x1, loops' own time, attend(): result, _ = lax.scan(advance, running, (key_split, value_split, pos_split))  3.67 us
  transfers between devices with their start and end apart: 2, of which 2 were waited for; matrix products, arithmetic and copies ran while one was open for 5% of the time, Pallas kernels for 0%

commit v1 on v0

--- a/solution.py
+++ b/solution.py
@@ -117,7 +117,12 @@
         jnp.zeros((kv_heads, group_dev, query_dev, head_dim), jnp.float32),
     )
     key_piece = lax.all_gather(key_rows, "blk", axis=0, tiled=True)
-    value_piece = lax.all_gather(value_rows, "blk", axis=0, tiled=True)
+    ring = [value_rows]
+    for hop in range(3):
+        ring.append(lax.ppermute(ring[-1], "blk", [(dev, (dev + 1) % 4) for dev in range(4)]))
+    value_piece = jnp.roll(
+        jnp.concatenate(ring[::-1], axis=0), (lax.axis_index("blk") + 1) * ring[0].shape[0], axis=0
+    )
     piece_pos = key_positions(
         key_piece.shape[0], shard_rows, prefix_dev, query_dev, block_order, block_count
     )

time: 161 us -> 144 us (0.89)
  the two profiles are of different devices: /device:TPU:0 before, /device:TPU:4 now
where the time goes in v1:
time: 144 us
  waiting for transfers between devices  54.6 us (38%)
  blocking collectives  21.9 us (15%)
  matrix products  19.7 us (14%)
  between operations  16.1 us (11%)
  other arithmetic  13.2 us (9%)
  local copies, waits for them, and re-layouts  12.6 us (9%)
  loops' own time  3.84 us (3%)
  starting transfers between devices  1.63 us (1%)
    ppermute x3, waiting for transfers between devices, on_device(): lax.ppermute(ring[-1], 'blk', [(dev, (dev + 1) % 4) for dev in range(4)])  41 us
    psum x1, blocking collectives, on_device(): latent = lax.psum(partial_latent, ('team', 'head')).astype(jnp.bfloat16)  21.9 us
    all_gather x1, waiting for transfers between devices, on_device(): key_piece = lax.all_gather(key_rows, 'blk', axis=0, tiled=True)  13.6 us
    dot_general x3, matrix products, compute(): jnp.einsum('kgts,skd->kgtd', weights.astype(jnp.bfloat16), block_values,...  12.1 us
    reduce_sum x3, other arithmetic, compute(): row_sum = row_sum * factor + jnp.sum(weights, axis=-1)  6.09 us
    unnamed x22, local copies, waits for them, and re-layouts  5.3 us
    dot_general x3, matrix products, compute(): jnp.einsum('tkgd,skd->kgts', query_rows, block_keys, preferred_element_ty...  4.2 us
    another operation x1, loops' own time, attend(): result, _ = lax.scan(advance, running, (key_split, value_split, pos_split))  3.61 us
  transfers between devices with their start and end apart: 4, of which 4 were waited for; matrix products, arithmetic and copies ran while one was open for 5% of the time, Pallas kernels for 0%

profile of v1, /device:TPU:4, one launch (start us, length us, event | category | flops | bytes accessed | tf_op | source)
XLA Modules:
  0.0 143.7 jit_solution(11553107753300940171)
XLA Ops:
  6.6 1.3 dynamic_slice.43
  9.8 1.2 convolution_bitcast_fusion
  11.0 21.9 %psum.7 = bf16[256,64]{0,1:T(8,128)(2,1)S(1)} all-reduce(f32[256,64]{0,1:T(8,128)S(1)} %convolution_bitcast_fusion), channel_id=1, replica_groups=mesh['team'=2,'blk'=4,'head'=4] {'team','head'}, use_global_device_ids=true, to_apply=%region_0.1 | all-reduce | flops 16384 | bytes 98304 | tf_op jit(solution)/shard_map/psum | solution.py:98
  32.9 1.0 copy.42
  33.9 0.8 constant_dynamic-slice_fusion.2
  34.7 1.1 fusion.22
  35.9 1.6 %collective-permute-start = (bf16[768,2,128]{2,0,1:T(8,128)(2,1)S(1)}, bf16[768,2,128]{2,0,1:T(8,128)(2,1)S(1)}, u32[]{:S(2)}, u32[]{:S(2)}) collective-permute-start(bf16[768,2,128]{2,0,1:T(8,128)(2,1)S(1)} %pad_maximum_fusion.1), channel_id=1, source_target_pairs={{0,4},{4,8},{8,12},{12,0},{1,5},{5,9},{9,13},{13,1},{2,6},{6,10},{... | collective-permute-start | bytes 1179656 | tf_op jit(solution)/shard_map/ppermute | solution.py:122
  37.5 12.0 %collective-permute-done = bf16[768,2,128]{2,0,1:T(8,128)(2,1)S(1)} collective-permute-done((bf16[768,2,128]{2,0,1:T(8,128)(2,1)S(1)}, bf16[768,2,128]{2,0,1:T(8,128)(2,1)S(1)}, u32[]{:S(2)}, u32[]{:S(2)}) %collective-permute-start) | collective-permute-done | bytes 393248 | tf_op jit(solution)/shard_map/ppermute | solution.py:122
  49.6 1.1 fusion.21
  50.7 1.0 copy.39
  51.7 0.8 pad_maximum_fusion
  52.5 0.6 dynamic_slice.42
  53.7 0.6 add_reduce_fusion
  54.3 0.1 copy.46
  54.4 0.1 select_reduce_fusion
  54.5 7.8 %collective-permute-done.1 = bf16[768,2,128]{2,0,1:T(8,128)(2,1)S(1)} collective-permute-done((bf16[768,2,128]{2,0,1:T(8,128)(2,1)S(1)}, bf16[768,2,128]{2,0,1:T(8,128)(2,1)S(1)}, u32[]{:S(2)}, u32[]{:S(2)}) %collective-permute-start.1) | collective-permute-done | bytes 393248 | tf_op jit(solution)/shard_map/ppermute | solution.py:122
  62.4 21.2 %collective-permute-done.2 = bf16[768,2,128]{2,0,1:T(8,128)(2,1)S(1)} collective-permute-done((bf16[768,2,128]{2,0,1:T(8,128)(2,1)S(1)}, bf16[768,2,128]{2,0,1:T(8,128)(2,1)S(1)}, u32[]{:S(2)}, u32[]{:S(2)}) %collective-permute-start.2) | collective-permute-done | bytes 393248 | tf_op jit(solution)/shard_map/ppermute | solution.py:122
  83.8 0.1 constant_dynamic-update-slice_fusion.6
  84.0 0.1 constant_dynamic-update-slice_fusion.1
  84.1 0.4 constant_dynamic-slice_fusion.1
  84.6 1.3 copy.47
  85.8 13.6 %all-gather.2.cloned.1.call-done = bf16[3072,2,128]{2,0,1:T(8,128)(2,1)} async-done(((bf16[768,2,128]{2,0,1:T(8,128)(2,1)}), bf16[3072,2,128]{2,0,1:T(8,128)(2,1)}) %all-gather.2.cloned.1.call-update) | async-done | bytes 1572880 | tf_op jit(solution)/shard_map/all_gather | solution.py:119
  99.4 1.5 %copy.45 = bf16[3,1024,2,128]{3,1,2,0:T(8,128)(2,1)S(1)} copy(bf16[3,1024,2,128]{3,1,0,2:T(8,128)(2,1)} %bitcast.83) | data formatting | bytes 3145728
  100.9 1.1 broadcast_in_dim.56
  102.0 31.8 %while.15 = (s32[]{:T(128)}, f32[2,4,256]{2,1,0:T(4,128)S(1)}, f32[2,4,256]{2,1,0:T(4,128)S(1)}, f32[2,4,256,128]{3,2,1,0:T(8,128)}, s32[3,1024]{1,0:T(4,128)S(1...) while((s32[]{:T(128)}, f32[2,4,256]{2,1,0:T(4,128)S(1)}, ...), condition=%wide.region_9.10_spmd.clone, body=%wide.region_3.9_spmd.clone.sunk | while | flops 1101796608 | bytes 38421312 | solution.py:69
  102.0 0.6 fusion.45
  103.8 8.7 %conditional.3 = (f32[2,4,256]{2,1,0:T(4,128)S(1)}, f32[2,4,256]{2,1,0:T(4,128)S(1)}, f32[2,4,256,128]{3,2,1,0:T(8,128)}) conditional(s32[]{:T(128)} %convert_element_type.57, (s32[1,1024]{1,0:T(1,128)S(1)}, s32[]{:T(128)}, bf16[3,1024,2,128]{3,1,2,0:T(8,128)(2,1)S(1)}, s32[]{:T(128)}, bf16[256,2,4,128]{3,0,2,1:T(8,128)(2,1)S(1)}, ...), branch_computations={%region_5.7_spmd, %region_8.8_spmd} | conditional | flops 1101795584 | bytes 38395480 | solution.py:67
  103.8 0.2 broadcast_compare_fusion
  104.1 1.4 fusion.2
  105.5 2.0 %fusion.4 = f32[2,4,256]{2,1,0:T(4,128)S(1)} fusion(f32[2,1024,256,4]{2,1,3,0:T(8,128)S(1)} %get-tuple-element.228, f32[2,4,256]{2,1,0:T(4,128)S(1)} %max.4, pred[256,1024]{0,1:T(8,128)(4,1)S(1)} %broadcast_compare_fusion), kind=kLoop, calls=%fused_computation.5 | loop fusion | flops 10483712 | bytes 8667136 | tf_op jit(solution)/shard_map/while/body/eval_jaxpr/cond/branch_0_fun/reduce_sum | solution.py:57
  107.5 4.0 %fusion.8 = f32[2,4,256,128]{3,2,1,0:T(8,128)S(1)} fusion(f32[2,1024,256,4]{2,1,3,0:T(8,128)S(1)} %get-tuple-element.228, f32[2,4,256]{2,1,0:T(4,128)S(1)} %max.4, pred[256,1024]{0,1:T(8,128)(4,1)S(1)} %broadcast_compare_fusion, f32[2,4,256,128]{3,2,1,0:T(8,128)S(1)} %copy-done.1, bf16[3,1024,2,128]{3,1,2,0:T(8,128)(2,1)} %get-tuple-element.125, ...), kind=kOutput, calls=%fused_computation.8 | convolution fusion | flops 547880960 | bytes 11289088 | tf_op jit(solution)/shard_map/while/body/eval_jaxpr/cond/branch_0_fun/kgts,skd->kgtd/dot_general | solution.py:58
  111.6 1.0 copy-done.2
  112.5 0.6 fusion.45
  114.4 8.7 %conditional.3 = (f32[2,4,256]{2,1,0:T(4,128)S(1)}, f32[2,4,256]{2,1,0:T(4,128)S(1)}, f32[2,4,256,128]{3,2,1,0:T(8,128)}) conditional(s32[]{:T(128)} %convert_element_type.57, (s32[1,1024]{1,0:T(1,128)S(1)}, s32[]{:T(128)}, bf16[3,1024,2,128]{3,1,2,0:T(8,128)(2,1)S(1)}, s32[]{:T(128)}, bf16[256,2,4,128]{3,0,2,1:T(8,128)(2,1)S(1)}, ...), branch_computations={%region_5.7_spmd, %region_8.8_spmd} | conditional | flops 1101795584 | bytes 38395480 | solution.py:67
  114.4 0.2 broadcast_compare_fusion
  114.6 1.4 fusion.2
  116.1 2.0 %fusion.4 = f32[2,4,256]{2,1,0:T(4,128)S(1)} fusion(f32[2,1024,256,4]{2,1,3,0:T(8,128)S(1)} %get-tuple-element.228, f32[2,4,256]{2,1,0:T(4,128)S(1)} %max.4, pred[256,1024]{0,1:T(8,128)(4,1)S(1)} %broadcast_compare_fusion), kind=kLoop, calls=%fused_computation.5 | loop fusion | flops 10483712 | bytes 8667136 | tf_op jit(solution)/shard_map/while/body/eval_jaxpr/cond/branch_0_fun/reduce_sum | solution.py:57
  118.1 4.0 %fusion.8 = f32[2,4,256,128]{3,2,1,0:T(8,128)S(1)} fusion(f32[2,1024,256,4]{2,1,3,0:T(8,128)S(1)} %get-tuple-element.228, f32[2,4,256]{2,1,0:T(4,128)S(1)} %max.4, pred[256,1024]{0,1:T(8,128)(4,1)S(1)} %broadcast_compare_fusion, f32[2,4,256,128]{3,2,1,0:T(8,128)S(1)} %copy-done.1, bf16[3,1024,2,128]{3,1,2,0:T(8,128)(2,1)} %get-tuple-element.125, ...), kind=kOutput, calls=%fused_computation.8 | convolution fusion | flops 547880960 | bytes 11289088 | tf_op jit(solution)/shard_map/while/body/eval_jaxpr/cond/branch_0_fun/kgts,skd->kgtd/dot_general | solution.py:58
  122.2 1.0 copy-done.2
  123.1 0.6 fusion.45
  125.0 8.7 %conditional.3 = (f32[2,4,256]{2,1,0:T(4,128)S(1)}, f32[2,4,256]{2,1,0:T(4,128)S(1)}, f32[2,4,256,128]{3,2,1,0:T(8,128)}) conditional(s32[]{:T(128)} %convert_element_type.57, (s32[1,1024]{1,0:T(1,128)S(1)}, s32[]{:T(128)}, bf16[3,1024,2,128]{3,1,2,0:T(8,128)(2,1)S(1)}, s32[]{:T(128)}, bf16[256,2,4,128]{3,0,2,1:T(8,128)(2,1)S(1)}, ...), branch_computations={%region_5.7_spmd, %region_8.8_spmd} | conditional | flops 1101795584 | bytes 38395480 | solution.py:67
  125.0 0.2 broadcast_compare_fusion
  125.2 1.4 fusion.2
  126.7 2.0 %fusion.4 = f32[2,4,256]{2,1,0:T(4,128)S(1)} fusion(f32[2,1024,256,4]{2,1,3,0:T(8,128)S(1)} %get-tuple-element.228, f32[2,4,256]{2,1,0:T(4,128)S(1)} %max.4, pred[256,1024]{0,1:T(8,128)(4,1)S(1)} %broadcast_compare_fusion), kind=kLoop, calls=%fused_computation.5 | loop fusion | flops 10483712 | bytes 8667136 | tf_op jit(solution)/shard_map/while/body/eval_jaxpr/cond/branch_0_fun/reduce_sum | solution.py:57
  128.7 4.0 %fusion.8 = f32[2,4,256,128]{3,2,1,0:T(8,128)S(1)} fusion(f32[2,1024,256,4]{2,1,3,0:T(8,128)S(1)} %get-tuple-element.228, f32[2,4,256]{2,1,0:T(4,128)S(1)} %max.4, pred[256,1024]{0,1:T(8,128)(4,1)S(1)} %broadcast_compare_fusion, f32[2,4,256,128]{3,2,1,0:T(8,128)S(1)} %copy-done.1, bf16[3,1024,2,128]{3,1,2,0:T(8,128)(2,1)} %get-tuple-element.125, ...), kind=kOutput, calls=%fused_computation.8 | convolution fusion | flops 547880960 | bytes 11289088 | tf_op jit(solution)/shard_map/while/body/eval_jaxpr/cond/branch_0_fun/kgts,skd->kgtd/dot_general | solution.py:58
  132.8 1.0 copy-done.2
  133.7 0.2 copy.48
  133.9 2.9 %fusion.24 = bf16[256,2,4,128]{3,2,1,0:T(4,128)(2,1)} fusion(f32[2,4,256]{1,0,2:T(2,128)S(1)} %copy.48, f32[2,4,256,128]{3,2,1,0:T(8,128)} %get-tuple-element.142), kind=kLoop, calls=%fused_computation.31 | loop fusion | flops 524288 | bytes 1581056 | tf_op jit(solution)/shard_map/convert_element_type | solution.py:133
  (51 shorter events, 0.6 us)
Async XLA Ops:
  6.5 3.3 %copy-start = (bf16[256,1024]{1,0:T(8,128)(2,1)S(1)}, bf16[256,1024]{1,0:T(8,128)(2,1)}, u32[]{:S(2)}) copy-start(bf16[256,1024]{1,0:T(8,128)(2,1)} %param.16) | copy-start | bytes 1572868
  6.5 46.0 %copy-start.5 = (s32[4]{0:T(128)S(1)}, s32[4]{0:T(128)}, u32[]{:S(2)}) copy-start(s32[4]{0:T(128)} %param.25) | copy-start | bytes 52
  6.5 47.7 %copy-start.4 = (bf16[256,2,4,128]{3,2,1,0:T(4,128)(2,1)S(1)}, bf16[256,2,4,128]{3,2,1,0:T(4,128)(2,1)}, u32[]{:S(2)}) copy-start(bf16[256,2,4,128]{3,2,1,0:T(4,128)(2,1)} %param.15) | copy-start | bytes 1572868
  6.5 92.9 %all-gather.2.cloned.1.call-start = ((), (), s32[]{:S(2)}) async-start(), calls=%async_computation | async-start | bytes 1966080 | tf_op jit(solution)/shard_map/all_gather | solution.py:119
  35.9 47.9 %copy-start.3 = (bf16[512,2,128]{2,1,0:T(2,128)(2,1)S(1)}, bf16[512,2,128]{2,1,0:T(2,128)(2,1)}, u32[]{:S(2)}) copy-start(bf16[512,2,128]{2,1,0:T(2,128)(2,1)} %param.23) | copy-start | bytes 786436
  35.9 13.6 %collective-permute-start = (bf16[768,2,128]{2,0,1:T(8,128)(2,1)S(1)}, bf16[768,2,128]{2,0,1:T(8,128)(2,1)S(1)}, u32[]{:S(2)}, u32[]{:S(2)}) collective-permute-start(bf16[768,2,128]{2,0,1:T(8,128)(2,1)S(1)} %pad_maximum_fusion.1), channel_id=1, source_target_pairs={{0,4},{4,8},{8,12},{12,0},{1,5},{5,9},{9,13},{13,1},{2,6},{6,10},{... | collective-permute-start | bytes 1179656 | tf_op jit(solution)/shard_map/ppermute | solution.py:122
  49.6 12.7 %collective-permute-start.1 = (bf16[768,2,128]{2,0,1:T(8,128)(2,1)S(1)}, bf16[768,2,128]{2,0,1:T(8,128)(2,1)S(1)}, u32[]{:S(2)}, u32[]{:S(2)}) collective-permute-start(bf16[768,2,128]{2,0,1:T(8,128)(2,1)S(1)} %collective-permute-done), channel_id=1, source_target_pairs={{0,4},{4,8},{8,12},{12,0},{1,5},{5,9},{9,13},{13,1},{2,6},{6,10},{... | collective-permute-start | bytes 1179656 | tf_op jit(solution)/shard_map/ppermute | solution.py:122
  62.3 21.3 %collective-permute-start.2 = (bf16[768,2,128]{2,0,1:T(8,128)(2,1)S(1)}, bf16[768,2,128]{2,0,1:T(8,128)(2,1)S(1)}, u32[]{:S(2)}, u32[]{:S(2)}) collective-permute-start(bf16[768,2,128]{2,0,1:T(8,128)(2,1)S(1)} %collective-permute-done.1), channel_id=1, source_target_pairs={{0,4},{4,8},{8,12},{12,0},{1,5},{5,9},{9,13},{13,1},{2,6},{6,10},{... | collective-permute-start | bytes 1179656 | tf_op jit(solution)/shard_map/ppermute | solution.py:122
  105.5 2.1 %copy-start.1 = (f32[2,4,256,128]{3,2,1,0:T(8,128)S(1)}, f32[2,4,256,128]{3,2,1,0:T(8,128)}, u32[]{:S(2)}) copy-start(f32[2,4,256,128]{3,2,1,0:T(8,128)} %get-tuple-element.124) | copy-start | bytes 3145732 | tf_op jit(solution)/shard_map/while/body/eval_jaxpr/cond
  111.6 1.0 copy-start.2
  116.1 2.1 %copy-start.1 = (f32[2,4,256,128]{3,2,1,0:T(8,128)S(1)}, f32[2,4,256,128]{3,2,1,0:T(8,128)}, u32[]{:S(2)}) copy-start(f32[2,4,256,128]{3,2,1,0:T(8,128)} %get-tuple-element.124) | copy-start | bytes 3145732 | tf_op jit(solution)/shard_map/while/body/eval_jaxpr/cond
  122.2 1.0 copy-start.2
  126.6 2.1 %copy-start.1 = (f32[2,4,256,128]{3,2,1,0:T(8,128)S(1)}, f32[2,4,256,128]{3,2,1,0:T(8,128)}, u32[]{:S(2)}) copy-start(f32[2,4,256,128]{3,2,1,0:T(8,128)} %get-tuple-element.124) | copy-start | bytes 3145732 | tf_op jit(solution)/shard_map/while/body/eval_jaxpr/cond
  132.8 1.0 copy-start.2
Sparse Core Ops, SparseCore 0:
  52.6 46.7 all-gather.1
